TPU v7x, 128 devices: a whole 4x4x4 slice. The times are simulated.
128 devices in a mesh: item: 4 (over z), user: 32 (over y, x, core).
Axes of the slice: x: 4, y: 4, z: 4, core: 2. Of those that a mesh axis runs over, the one named last changes fastest.
Arguments:
- interactions: bfloat16 [65536, 16384], P('user', 'item'), may hold values from 0 to 1, as said below
- omega: float32 [16384, 256], P('item'), may hold values from -6 to 6
Outputs:
- scaled_basis: float32 [16384, 256], P('item')
Inputs may be any that keep to these rules, and one draw needn't show every extreme that they name: `interactions`: every entry is 0 or 1.
All inputs are finite; a program needn't handle non-finite values.
Results may differ from a plain program's by a relative error of at most 0.0003.
Values sent between devices are 32-bit elements; how exact they have to be, the bound alone decides.
No kernel may reach another device: no remote copies, remote signals or barrier semaphores. Data moves between devices by JAX's collectives and lax.ppermute only.
A program may use at most 128 MiB of HBM per device.

v0:
```python
import jax
import jax.numpy as jnp
from jax import lax
from jax.sharding import PartitionSpec as P

ridge = 200.0
highest = lax.Precision.HIGHEST


def gram_of(block):
    return lax.dot_general(
        block,
        block,
        (((0,), (0,)), ((), ())),
        precision=highest,
        preferred_element_type=jnp.float32,
    )


def factor(block, gram):
    lower = jnp.linalg.cholesky(gram)
    return lax.linalg.triangular_solve(lower, block, left_side=False, lower=True, transpose_a=True)


def gram_wide(block):
    return lax.psum(gram_of(block), ("item", "user"))


def local(interactions, omega):
    local_rows = jnp.dot(interactions, omega, precision=highest, preferred_element_type=jnp.float32)
    user_sketch = lax.psum(local_rows, "item")
    item_count = omega.shape[0] * lax.axis_size("item")
    factor_scale = jnp.sqrt(jnp.float32(item_count))
    own_rows = omega.shape[0] // lax.axis_size("user")
    block = lax.psum_scatter(
        lax.dot_general(
            interactions,
            user_sketch,
            (((0,), (0,)), ((), ())),
            precision=highest,
            preferred_element_type=jnp.float32,
        ),
        "user",
        scatter_dimension=0,
        tiled=True,
    )
    own_omega = lax.dynamic_slice_in_dim(omega, lax.axis_index("user") * own_rows, own_rows, 0)
    block = block + ridge * own_omega
    for sweep in range(2):
        block = factor(block, gram_wide(block))
    return lax.all_gather(factor_scale * block, "user", axis=0, tiled=True)


def solution(mesh):
    in_specs = (P("user", "item"), P("item", None))
    out_specs = P("item", None)
    return jax.shard_map(local, mesh=mesh, in_specs=in_specs, out_specs=out_specs, check_vma=False)
```

profile of v0, /device:TPU:1, one launch (start us, length us, event | category | flops | bytes accessed | tf_op | source)
XLA Modules:
  0.0 661.8 jit_solution(2004291830693291663)
XLA Ops:
  6.5 18.5 %fusion.27 = f32[2048,256]{1,0:T(8,128)} fusion(bf16[2048,4096]{1,0:T(8,128)(2,1)} %param.5, f32[4096,256]{1,0:T(8,128)} %param.6), kind=kOutput, calls=%fused_computation.63 | convolution fusion | flops 25769803776 | bytes 23068672 | tf_op jit(solution)/shard_map/dot_general | solution.py:30
  25.1 62.1 %all-reduce.5.cloned.1.call-done = f32[2048,256]{1,0:T(8,128)} async-done(((f32[2048,256]{1,0:T(8,128)}), f32[2048,256]{1,0:T(8,128)}) %all-reduce.5.cloned.1.call-update) | async-done | bytes 2097168 | tf_op jit(solution)/shard_map/psum | solution.py:31
  87.2 17.8 %convolution_bitcast_fusion = f32[4096,256]{0,1:T(8,128)} fusion(f32[2048,256]{1,0:T(8,128)} %all-reduce.5.cloned.1.call-done, bf16[2048,4096]{1,0:T(8,128)(2,1)} %param.5), kind=kOutput, calls=%fused_computation.4 | convolution fusion | flops 25769803776 | bytes 23068672 | tf_op jit(solution)/shard_map/dot_general | solution.py:36
  106.1 79.4 %reduce-scatter.2.cloned.1.call-done = f32[128,256]{0,1:T(8,128)} async-done(((f32[4096,256]{0,1:T(8,128)}), f32[128,256]{0,1:T(8,128)}) %reduce-scatter.2.cloned.1.call-update) | async-done | bytes 131088 | tf_op jit(solution)/shard_map/reduce_scatter | solution.py:35
  186.4 1.1 fusion.28
  187.8 146.7 %all-reduce.7.cloned.1.call-done = f32[256,256]{0,1:T(8,128)} async-done(((f32[256,256]{0,1:T(8,128)}), f32[256,256]{0,1:T(8,128)}) %all-reduce.7.cloned.1.call-update) | async-done | bytes 262160 | tf_op jit(solution)/shard_map/psum | solution.py:26
  336.6 11.7 %cholesky.130 = f32[128,128]{1,0:T(8,128)S(1)} custom-call(f32[128,128]{1,0:T(8,128)S(1)} %cholesky.194), custom_call_target="Cholesky" | custom-call | tf_op jit(solution)/shard_map/jit(cholesky)/cholesky | solution.py:21
  348.3 9.8 %custom-call.13 = f32[1,128,128]{1,2,0:T(8,128)S(1)} custom-call(f32[1,128,128]{2,1,0:T(8,128)S(1)} %get-tuple-element.50), custom_call_target="InvertDiagBlocksLowerTriangular" | custom-call | tf_op jit(solution)/shard_map/jit(cholesky)/cholesky | solution.py:21
  358.6 11.7 %cholesky.147 = f32[128,128]{1,0:T(8,128)S(1)} custom-call(f32[128,128]{1,0:T(8,128)S(1)} %convolution_subtract_fusion.3), custom_call_target="Cholesky" | custom-call | tf_op jit(solution)/shard_map/jit(cholesky)/cholesky | solution.py:21
  372.6 4.1 while.4
  373.2 1.4 bitcast_dynamic-update-slice_fusion.4
  375.3 1.4 bitcast_dynamic-update-slice_fusion.4
  376.7 19.7 %custom-call.14 = f32[2,128,128]{1,2,0:T(8,128)S(1)} custom-call(f32[2,128,128]{2,1,0:T(8,128)S(1)} %get-tuple-element.21), custom_call_target="InvertDiagBlocksLowerTriangular" | custom-call | tf_op jit(solution)/shard_map/triangular_solve/custom-call.0 | solution.py:22
  397.2 1.1 fusion.2
  398.6 140.5 %all-reduce.9.cloned.1.call-done = f32[256,256]{0,1:T(8,128)} async-done(((f32[256,256]{0,1:T(8,128)}), f32[256,256]{0,1:T(8,128)}) %all-reduce.9.cloned.1.call-update) | async-done | bytes 262160 | tf_op jit(solution)/shard_map/psum | solution.py:26
  541.1 11.7 %cholesky.164 = f32[128,128]{1,0:T(8,128)S(1)} custom-call(f32[128,128]{1,0:T(8,128)S(1)} %cholesky.197), custom_call_target="Cholesky" | custom-call | tf_op jit(solution)/shard_map/jit(cholesky)/cholesky | solution.py:21
  553.5 9.8 %custom-call.15 = f32[1,128,128]{1,2,0:T(8,128)S(1)} custom-call(f32[1,128,128]{2,1,0:T(8,128)S(1)} %get-tuple-element.46), custom_call_target="InvertDiagBlocksLowerTriangular" | custom-call | tf_op jit(solution)/shard_map/jit(cholesky)/cholesky | solution.py:21
  563.8 11.7 %cholesky.181 = f32[128,128]{1,0:T(8,128)S(1)} custom-call(f32[128,128]{1,0:T(8,128)S(1)} %convolution_subtract_fusion.1), custom_call_target="Cholesky" | custom-call | tf_op jit(solution)/shard_map/jit(cholesky)/cholesky | solution.py:21
  577.7 4.4 while.5
  578.6 1.4 bitcast_dynamic-update-slice_fusion.5
  580.6 1.4 bitcast_dynamic-update-slice_fusion.5
  582.1 19.7 %custom-call.16 = f32[2,128,128]{1,2,0:T(8,128)S(1)} custom-call(f32[2,128,128]{2,1,0:T(8,128)S(1)} %get-tuple-element.22), custom_call_target="InvertDiagBlocksLowerTriangular" | custom-call | tf_op jit(solution)/shard_map/triangular_solve/custom-call.0 | solution.py:22
  603.3 46.4 %all-gather.2.cloned.1.call-done = f32[4096,256]{0,1:T(8,128)} async-done(((f32[128,256]{0,1:T(8,128)}), f32[4096,256]{0,1:T(8,128)}) %all-gather.2.cloned.1.call-update) | async-done | bytes 4194320 | tf_op jit(solution)/shard_map/all_gather | solution.py:51
  649.7 5.6 copy.8
  (53 shorter events, 14.7 us)
Async XLA Ops:
  6.5 80.7 %all-reduce.5.cloned.1.call-start = ((), (), s32[]{:S(2)}) async-start(), calls=%async_computation.1 | async-start | bytes 4194304 | tf_op jit(solution)/shard_map/psum | solution.py:31
  25.1 160.4 %reduce-scatter.2.cloned.1.call-start = ((), (), s32[]{:S(2)}) async-start(), calls=%async_computation.2 | async-start | bytes 4325376 | tf_op jit(solution)/shard_map/reduce_scatter | solution.py:35
  105.0 229.5 %all-reduce.7.cloned.1.call-start = ((), (), s32[]{:S(2)}) async-start(), calls=%async_computation.3 | async-start | bytes 524288 | tf_op jit(solution)/shard_map/psum | solution.py:26
  187.5 351.5 %all-reduce.9.cloned.1.call-start = ((), (), s32[]{:S(2)}) async-start(), calls=%async_computation.4 | async-start | bytes 524288 | tf_op jit(solution)/shard_map/psum | solution.py:26
  398.3 251.4 %all-gather.2.cloned.1.call-start = ((), (), s32[]{:S(2)}) async-start(), calls=%async_computation.5 | async-start | bytes 4325376 | tf_op jit(solution)/shard_map/all_gather | solution.py:51
Sparse Core Ops, SparseCore 0:
  25.2 61.9 all-reduce.4
  105.1 80.3 reduce-scatter.1
  190.3 144.1 all-reduce.6
  398.4 140.5 all-reduce.8
  603.4 46.2 all-gather.1
where the time goes:
time: 662 us
  waiting for transfers between devices  475 us (72%)
  other arithmetic  112 us (17%)
  matrix products  40.9 us (6%)
  local copies, waits for them, and re-layouts  17 us (3%)
  between operations  16 us (2%)
    psum x2, waiting for transfers between devices, gram_wide(): return lax.psum(gram_of(block), ('item', 'user'))  287 us
    reduce_scatter x1, waiting for transfers between devices, local(): lax.psum_scatter(lax.dot_general(interactions, user_sketch, (((0,), (0,))...  79.4 us
    another operation x13, other arithmetic, factor(): lower = jnp.linalg.cholesky(gram)  68.7 us
    psum x1, waiting for transfers between devices, local(): user_sketch = lax.psum(local_rows, 'item')  62.1 us
    all_gather x1, waiting for transfers between devices, local(): return lax.all_gather(factor_scale * block, 'user', axis=0, tiled=True)  46.4 us
    another operation x5, other arithmetic, factor(): lax.linalg.triangular_solve(lower, block, left_side=False, lower=True, tr...  39.4 us
    dot_general x1, matrix products, local(): jnp.dot(interactions, omega, precision=highest, preferred_element_type=jn...  18.5 us
    dot_general x1, matrix products, local(): lax.dot_general(interactions, user_sketch, (((0,), (0,)), ((), ())), prec...  17.8 us
  transfers between devices with their start and end apart: 5, of which 5 were waited for; matrix products, arithmetic and copies ran while one was open for 0% of the time, Pallas kernels for 0%

commit v1 on v0

--- a/solution.py
+++ b/solution.py
@@ -5,6 +5,12 @@
 
 ridge = 200.0
 highest = lax.Precision.HIGHEST
+
+
+def pools_find(u):
+    arr_out = lax.all_gather(u, axis_name=("item", "user"))
+    part_next = jnp.sum(arr_out, axis=0)
+    return part_next
 
 
 def gram_of(block):
@@ -23,7 +29,7 @@
 
 
 def gram_wide(block):
-    return lax.psum(gram_of(block), ("item", "user"))
+    return pools_find(gram_of(block))
 
 
 def local(interactions, omega):

time: 662 us -> 611 us (0.923)
  waiting for transfers between devices: 475 us -> 404 us
  other arithmetic: 112 us -> 134 us
    psum x2 -> x0, waiting for transfers between devices: 287 us -> none  [gram_wide(): return lax.psum(gram_of(block), ('item', 'user'))]
    all_gather x0 -> x2, waiting for transfers between devices: none -> 214 us  [pools_find(): arr_out = lax.all_gather(u, axis_name=('item', 'user'))]
    reduce_sum x0 -> x2, other arithmetic: none -> 24 us  [pools_find(): part_next = jnp.sum(arr_out, axis=0)]
where the time goes in v1:
time: 611 us
  waiting for transfers between devices  404 us (66%)
  other arithmetic  134 us (22%)
  matrix products  40.9 us (7%)
  between operations  16.1 us (3%)
  local copies, waits for them, and re-layouts  15.1 us (2%)
    all_gather x2, waiting for transfers between devices, pools_find(): arr_out = lax.all_gather(u, axis_name=('item', 'user'))  214 us
    reduce_scatter x1, waiting for transfers between devices, local(): lax.psum_scatter(lax.dot_general(interactions, user_sketch, (((0,), (0,))...  79.4 us
    another operation x13, other arithmetic, factor(): lower = jnp.linalg.cholesky(gram)  68.7 us
    psum x1, waiting for transfers between devices, local(): user_sketch = lax.psum(local_rows, 'item')  62.1 us
    all_gather x1, waiting for transfers between devices, local(): return lax.all_gather(factor_scale * block, 'user', axis=0, tiled=True)  47.9 us
    another operation x5, other arithmetic, factor(): lax.linalg.triangular_solve(lower, block, left_side=False, lower=True, tr...  39.9 us
    reduce_sum x2, other arithmetic, pools_find(): part_next = jnp.sum(arr_out, axis=0)  24 us
    dot_general x1, matrix products, local(): jnp.dot(interactions, omega, precision=highest, preferred_element_type=jn...  18.5 us
  transfers between devices with their start and end apart: 5, of which 5 were waited for; matrix products, arithmetic and copies ran while one was open for 0% of the time, Pallas kernels for 0%

profile of v1, /device:TPU:1, one launch (start us, length us, event | category | flops | bytes accessed | tf_op | source)
XLA Modules:
  0.0 610.6 jit_solution(2706185334762135721)
XLA Ops:
  6.5 18.5 %fusion.27 = f32[2048,256]{1,0:T(8,128)} fusion(bf16[2048,4096]{1,0:T(8,128)(2,1)} %param.5, f32[4096,256]{1,0:T(8,128)} %param.6), kind=kOutput, calls=%fused_computation.63 | convolution fusion | flops 25769803776 | bytes 23068672 | tf_op jit(solution)/shard_map/dot_general | solution.py:36
  25.1 62.1 %all-reduce.3.cloned.1.call-done = f32[2048,256]{1,0:T(8,128)} async-done(((f32[2048,256]{1,0:T(8,128)}), f32[2048,256]{1,0:T(8,128)}) %all-reduce.3.cloned.1.call-update) | async-done | bytes 2097168 | tf_op jit(solution)/shard_map/psum | solution.py:37
  87.2 17.8 %convolution_bitcast_fusion = f32[4096,256]{0,1:T(8,128)} fusion(f32[2048,256]{1,0:T(8,128)} %all-reduce.3.cloned.1.call-done, bf16[2048,4096]{1,0:T(8,128)(2,1)} %param.5), kind=kOutput, calls=%fused_computation.4 | convolution fusion | flops 25769803776 | bytes 23068672 | tf_op jit(solution)/shard_map/dot_general | solution.py:42
  106.1 79.4 %reduce-scatter.2.cloned.1.call-done = f32[128,256]{0,1:T(8,128)} async-done(((f32[4096,256]{0,1:T(8,128)}), f32[128,256]{0,1:T(8,128)}) %reduce-scatter.2.cloned.1.call-update) | async-done | bytes 131088 | tf_op jit(solution)/shard_map/reduce_scatter | solution.py:41
  187.8 108.5 %all-gather.8.cloned.1.call-done = f32[32768,256]{1,0:T(8,128)} async-done(((f32[256,256]{1,0:T(8,128)}), f32[32768,256]{1,0:T(8,128)}) %all-gather.8.cloned.1.call-update) | async-done | bytes 33554448 | tf_op jit(solution)/shard_map/all_gather | solution.py:11
  296.3 12.0 %reduce_sum.18 = f32[256,256]{1,0:T(8,128)S(1)} reduce(f32[128,256,256]{2,1,0:T(8,128)} %bitcast.76, f32[]{:T(128)} %constant.69.clone.1), dimensions={0}, to_apply=%region_2.0 | reduce | flops 8323072 | bytes 33816580 | tf_op jit(solution)/shard_map/reduce_sum | solution.py:12
  308.5 11.7 %cholesky.130 = f32[128,128]{1,0:T(8,128)S(1)} custom-call(f32[128,128]{1,0:T(8,128)S(1)} %cholesky.194), custom_call_target="Cholesky" | custom-call | tf_op jit(solution)/shard_map/jit(cholesky)/cholesky | solution.py:27
  320.2 9.8 %custom-call.13 = f32[1,128,128]{1,2,0:T(8,128)S(1)} custom-call(f32[1,128,128]{2,1,0:T(8,128)S(1)} %get-tuple-element.50), custom_call_target="InvertDiagBlocksLowerTriangular" | custom-call | tf_op jit(solution)/shard_map/jit(cholesky)/cholesky | solution.py:27
  330.6 11.7 %cholesky.147 = f32[128,128]{1,0:T(8,128)S(1)} custom-call(f32[128,128]{1,0:T(8,128)S(1)} %convolution_subtract_fusion.3), custom_call_target="Cholesky" | custom-call | tf_op jit(solution)/shard_map/jit(cholesky)/cholesky | solution.py:27
  344.5 4.1 while.4
  345.1 1.4 bitcast_dynamic-update-slice_fusion.4
  347.2 1.4 bitcast_dynamic-update-slice_fusion.4
  348.6 19.9 %custom-call.14 = f32[2,128,128]{1,2,0:T(8,128)S(1)} custom-call(f32[2,128,128]{2,1,0:T(8,128)S(1)} %get-tuple-element.21), custom_call_target="InvertDiagBlocksLowerTriangular" | custom-call | tf_op jit(solution)/shard_map/triangular_solve/custom-call.0 | solution.py:28
  370.5 105.8 %all-gather.10.cloned.1.call-done = f32[32768,256]{1,0:T(8,128)} async-done(((f32[256,256]{1,0:T(8,128)}), f32[32768,256]{1,0:T(8,128)}) %all-gather.10.cloned.1.call-update) | async-done | bytes 33554448 | tf_op jit(solution)/shard_map/all_gather | solution.py:11
  476.3 12.0 %reduce_sum.19 = f32[256,256]{1,0:T(8,128)S(1)} reduce(f32[128,256,256]{2,1,0:T(8,128)} %bitcast.77, f32[]{:T(128)} %constant.69.clone.1), dimensions={0}, to_apply=%region_7.10 | reduce | flops 8323072 | bytes 33816580 | tf_op jit(solution)/shard_map/reduce_sum | solution.py:12
  488.4 11.7 %cholesky.164 = f32[128,128]{1,0:T(8,128)S(1)} custom-call(f32[128,128]{1,0:T(8,128)S(1)} %cholesky.197), custom_call_target="Cholesky" | custom-call | tf_op jit(solution)/shard_map/jit(cholesky)/cholesky | solution.py:27
  500.2 9.8 %custom-call.15 = f32[1,128,128]{1,2,0:T(8,128)S(1)} custom-call(f32[1,128,128]{2,1,0:T(8,128)S(1)} %get-tuple-element.46), custom_call_target="InvertDiagBlocksLowerTriangular" | custom-call | tf_op jit(solution)/shard_map/jit(cholesky)/cholesky | solution.py:27
  510.5 11.7 %cholesky.181 = f32[128,128]{1,0:T(8,128)S(1)} custom-call(f32[128,128]{1,0:T(8,128)S(1)} %convolution_subtract_fusion.1), custom_call_target="Cholesky" | custom-call | tf_op jit(solution)/shard_map/jit(cholesky)/cholesky | solution.py:27
  525.0 4.1 while.5
  525.6 1.4 bitcast_dynamic-update-slice_fusion.5
  527.7 1.4 bitcast_dynamic-update-slice_fusion.5
  529.1 19.9 %custom-call.16 = f32[2,128,128]{1,2,0:T(8,128)S(1)} custom-call(f32[2,128,128]{2,1,0:T(8,128)S(1)} %get-tuple-element.22), custom_call_target="InvertDiagBlocksLowerTriangular" | custom-call | tf_op jit(solution)/shard_map/triangular_solve/custom-call.0 | solution.py:28
  550.5 47.9 %all-gather.6.cloned.1.call-done = f32[4096,256]{0,1:T(8,128)} async-done(((f32[128,256]{0,1:T(8,128)}), f32[4096,256]{0,1:T(8,128)}) %all-gather.6.cloned.1.call-update) | async-done | bytes 4194320 | tf_op jit(solution)/shard_map/all_gather | solution.py:57
  598.5 5.6 copy.10
  (55 shorter events, 12.8 us)
Async XLA Ops:
  6.5 80.7 %all-reduce.3.cloned.1.call-start = ((), (), s32[]{:S(2)}) async-start(), calls=%async_computation.1 | async-start | bytes 4194304 | tf_op jit(solution)/shard_map/psum | solution.py:37
  25.1 160.4 %reduce-scatter.2.cloned.1.call-start = ((), (), s32[]{:S(2)}) async-start(), calls=%async_computation.2 | async-start | bytes 4325376 | tf_op jit(solution)/shard_map/reduce_scatter | solution.py:41
  105.0 191.3 %all-gather.8.cloned.1.call-start = ((), (), s32[]{:S(2)}) async-start(), calls=%async_computation.4 | async-start | bytes 33816576 | tf_op jit(solution)/shard_map/all_gather | solution.py:11
  187.5 288.7 %all-gather.10.cloned.1.call-start = ((), (), s32[]{:S(2)}) async-start(), calls=%async_computation.5 | async-start | bytes 33816576 | tf_op jit(solution)/shard_map/all_gather | solution.py:11
  370.4 228.0 %all-gather.6.cloned.1.call-start = ((), (), s32[]{:S(2)}) async-start(), calls=%async_computation.3 | async-start | bytes 4325376 | tf_op jit(solution)/shard_map/all_gather | solution.py:57
Sparse Core Ops, SparseCore 0:
  25.2 61.9 all-reduce.2
  105.1 80.3 reduce-scatter.1
  188.5 107.7 all-gather.7
  370.6 105.6 all-gather.9
  550.7 47.7 all-gather.5
